TPU v7x, 256 devices: a whole 4x4x8 slice. The times are simulated.
256 devices in a mesh: dp: 32 (over y, x, core), ctx: 8 (over z).
Axes of the slice: x: 4, y: 4, z: 8, core: 2. Of those that a mesh axis runs over, the one named last changes fastest.
Arguments:
- value: bfloat16 [32, 1024, 512], P('dp', 'ctx'), may hold values from -6 to 6
- gate_one: bfloat16 [32, 1024, 512], P('dp', 'ctx'), may hold values from -6 to 6
- gate_two: bfloat16 [32, 1024, 512], P('dp', 'ctx'), may hold values from -6 to 6
- filters: bfloat16 [2, 1024, 512], replicated, may hold values from -0.1875 to 0.1875
- out_weight: bfloat16 [512, 512], replicated, may hold values from -0.25 to 0.25
- grad_out: bfloat16 [32, 1024, 512], P('dp', 'ctx'), may hold values from -6 to 6
Outputs:
- mixed: bfloat16 [32, 1024, 512], P('dp', 'ctx')
- grad_value: bfloat16 [32, 1024, 512], P('dp', 'ctx')
- grad_gate_one: bfloat16 [32, 1024, 512], P('dp', 'ctx')
- grad_gate_two: bfloat16 [32, 1024, 512], P('dp', 'ctx')
- filter_grad: float32 [2, 1024, 512], P(None, 'ctx', 'dp')
- weight_grad: float32 [512, 512], P('dp', 'ctx')
All inputs are finite; a program needn't handle non-finite values.
Results may differ from a plain program's by a relative error of at most 0.019.
Values may be sent and summed in bfloat16 or wider, within the bound.
A program may use at most 128 MiB of HBM per device.

v0:
```python
import math
import jax
import jax.numpy as jnp
from jax import lax
from jax.sharding import PartitionSpec as P


def make_tables(block):
    period = 2 * block
    freq_bins = jnp.concatenate(
        [jnp.arange(block + 1, dtype=jnp.int32), jnp.arange(1, block, dtype=jnp.int32)]
    )
    sine_rows = jnp.arange(period, dtype=jnp.int32) > block
    inputs = jnp.arange(block, dtype=jnp.int32)
    turns = freq_bins[:, None] * inputs[None, :] % period
    radians = turns.astype(jnp.float32) * (2.0 * math.pi / period)
    forward = jnp.where(sine_rows[:, None], jnp.sin(radians), jnp.cos(radians))
    moments = jnp.arange(period, dtype=jnp.int32)
    turns_back = moments[:, None] * freq_bins[None, :] % period
    radians_back = turns_back.astype(jnp.float32) * (2.0 * math.pi / period)
    border_bins = (freq_bins == 0) | (freq_bins == block)
    weights = jnp.where(border_bins, 1.0, 2.0) / period
    inverse = (
        jnp.where(sine_rows[None, :], jnp.sin(radians_back), jnp.cos(radians_back))
        * weights[None, :]
    )
    parity = jnp.where(freq_bins % 2 == 0, 1.0, -1.0).astype(jnp.float32)[:, None]
    return (forward, inverse, parity)


def to_spectra(blocks, table):
    return jnp.einsum(
        "fb,...bd->...fd", table, blocks.astype(jnp.float32), precision=lax.Precision.HIGHEST
    )


def from_spectra(table, spectra):
    return jnp.einsum("tf,...fd->...td", table, spectra, precision=lax.Precision.HIGHEST)


def spectral_product(left, right, block, conj_left):
    left_real = left[..., : block + 1, :]
    left_imag = left[..., block + 1 :, :]
    right_real = right[..., : block + 1, :]
    right_imag = right[..., block + 1 :, :]
    if conj_left:
        left_imag = -left_imag
    cross = left_imag * right_imag
    border = jnp.zeros_like(cross[..., :1, :])
    real_part = left_real * right_real - jnp.concatenate([border, cross, border], axis=-2)
    imag_part = left_real[..., 1:block, :] * right_imag + left_imag * right_real[..., 1:block, :]
    return jnp.concatenate([real_part, imag_part], axis=-2)


def on_device(value, gate_one, gate_two, filters, out_weight, grad_out):
    rows = value.shape[1]
    width = value.shape[2]
    seq_count = lax.axis_size("ctx")
    data_count = lax.axis_size("dp")
    position = lax.axis_index("ctx")
    block = math.gcd(rows, 128)
    own_blocks = rows // block
    lag_blocks = own_blocks * seq_count
    forward, inverse, parity = make_tables(block)
    low_rows = inverse[:block]
    high_rows = inverse[block:]
    first_block = position * own_blocks
    own_start = position * rows
    filter_blocks = filters.reshape(2, lag_blocks, block, width)
    filter_spectra = to_spectra(filter_blocks, forward)
    padded_filters = jnp.concatenate([jnp.zeros_like(filter_spectra), filter_spectra], axis=1)

    def piece_spectra_of(piece):
        count = piece.shape[0] // block
        return to_spectra(piece.reshape(count, block, width), forward)

    def causal(source, padded_filter):
        initial = jnp.zeros((own_blocks + 1, 2 * block, width), jnp.float32)
        piece = lax.all_gather(source, "ctx", axis=0, tiled=True)
        start = jnp.int32(0)

        def work(total):
            piece_spectra = piece_spectra_of(piece)
            count = piece_spectra.shape[0]
            start_block = start // block
            last_block = start_block + count - 1
            terms_list = []
            for index in range(own_blocks + 1):
                out_block = first_block - 1 + index
                anchor = jnp.maximum(out_block, 0)
                window = lax.dynamic_slice_in_dim(
                    padded_filter, lag_blocks + anchor - last_block, count, 0
                )
                window = jnp.flip(window, 0)
                summed_term = jnp.sum(spectral_product(window, piece_spectra, block, False), axis=0)
                if index == 0:
                    summed_term = summed_term * (out_block >= 0).astype(jnp.float32)
                terms_list.append(summed_term)
            return total + jnp.stack(terms_list)

        summed = lax.cond(start < own_start + rows, work, lambda total: total, initial)
        lower = from_spectra(low_rows, summed[1:])
        upper = from_spectra(high_rows, summed[:-1])
        return (lower + upper).reshape(rows, width)

    def anti_owner(source, grad_rows, padded_filter):
        filter_spectrum = padded_filter[lag_blocks:]
        whole_source, whole_grad = (
            lax.all_gather(source, "ctx", axis=0, tiled=True),
            lax.all_gather(grad_rows, "ctx", axis=0, tiled=True),
        )
        source_spectra = piece_spectra_of(whole_source)
        grad_spectra = piece_spectra_of(whole_grad)
        following = (
            jnp.concatenate([grad_spectra[1:], jnp.zeros_like(grad_spectra[:1])], axis=0) * parity
        )
        combined = grad_spectra + following
        padded = jnp.concatenate([combined, jnp.zeros_like(combined)], axis=0)

        def one_block(offset):
            window = lax.dynamic_slice_in_dim(padded, offset, lag_blocks, 0)
            grad_piece = jnp.sum(spectral_product(filter_spectrum, window, block, True), axis=0)
            lag_piece = jnp.sum(spectral_product(source_spectra, window, block, True), axis=0)
            return (grad_piece, lag_piece)

        grad_parts, lag_parts = lax.map(
            one_block, first_block + jnp.arange(own_blocks, dtype=jnp.int32)
        )
        grad_part = from_spectra(low_rows, grad_parts).reshape(rows, width)
        lag_part = from_spectra(low_rows, lag_parts).reshape(rows, width)
        return (grad_part, lag_part)

    def backward(source, grad_rows, padded_filter):
        return anti_owner(source, grad_rows, padded_filter)

    value_rows = value[0]
    gate_first = gate_one[0].astype(jnp.float32)
    gate_second = gate_two[0].astype(jnp.float32)
    cotangent = grad_out[0]
    first_conv = causal(value_rows, padded_filters[0])
    mixed_input = (gate_first * first_conv).astype(jnp.bfloat16)
    second_conv = causal(mixed_input, padded_filters[1])
    gated = (gate_second * second_conv).astype(jnp.bfloat16)
    mixed = jnp.dot(gated, out_weight, preferred_element_type=jnp.float32).astype(jnp.bfloat16)
    grad_gated = lax.dot_general(
        cotangent, out_weight, (((1,), (1,)), ((), ())), preferred_element_type=jnp.float32
    )
    grad_gate_two = (grad_gated * second_conv).astype(jnp.bfloat16)
    grad_second = (grad_gated * gate_second).astype(jnp.bfloat16)
    grad_mixed, lag_second = backward(mixed_input, grad_second, padded_filters[1])
    grad_gate_one = (grad_mixed * first_conv).astype(jnp.bfloat16)
    grad_first = (grad_mixed * gate_first).astype(jnp.bfloat16)
    grad_value_full, lag_first = backward(value_rows, grad_first, padded_filters[0])
    grad_value = grad_value_full.astype(jnp.bfloat16)
    own_lags = jnp.stack([lag_first, lag_second])
    filter_grad = (
        lax.psum_scatter(
            own_lags.astype(jnp.bfloat16), "dp", scatter_dimension=2, tiled=True
        ).astype(jnp.float32)
        / data_count
    )
    weight_part = lax.psum_scatter(
        lax.dot_general(
            gated, cotangent, (((0,), (0,)), ((), ())), preferred_element_type=jnp.float32
        ).astype(jnp.bfloat16),
        "dp",
        scatter_dimension=0,
        tiled=True,
    )
    weight_grad = (
        lax.psum_scatter(weight_part, "ctx", scatter_dimension=1, tiled=True).astype(jnp.float32)
        / data_count
    )
    return (
        mixed[None],
        grad_value[None],
        grad_gate_one[None],
        grad_gate_two[None],
        filter_grad,
        weight_grad,
    )


def solution(mesh):
    return jax.shard_map(
        on_device,
        mesh=mesh,
        in_specs=(
            P("dp", "ctx", None),
            P("dp", "ctx", None),
            P("dp", "ctx", None),
            P(),
            P(),
            P("dp", "ctx", None),
        ),
        out_specs=(
            P("dp", "ctx", None),
            P("dp", "ctx", None),
            P("dp", "ctx", None),
            P("dp", "ctx", None),
            P(None, "ctx", "dp"),
            P("dp", "ctx"),
        ),
        check_vma=False,
    )
```

profile of v0, /device:TPU:2, one launch (start us, length us, event | category | flops | bytes accessed | tf_op | source)
XLA Modules:
  0.0 464.7 jit_solution(18322438985190754017)
XLA Ops:
  8.0 1.0 copy.24
  9.2 3.9 convolution_bitcast_fusion.2
  13.1 8.0 %concatenate.92 = f32[2,16,256,512]{3,2,1,0:T(8,128)} pad(f32[2,8,256,512]{3,2,1,0:T(8,128)S(1)} %convolution_bitcast_fusion.2, f32[]{:T(128)} %constant.162.clone.1), padding=0_0x8_0x0_0x0_0 | pad | bytes 25165828 | tf_op jit(solution)/shard_map/concatenate | solution.py:71
  21.4 1.3 cosine_select_fusion
  22.7 1.1 select_multiply_fusion
  23.7 27.5 %all-gather.10.cloned.1.call-done = bf16[1,1024,512]{2,1,0:T(8,128)(2,1)} async-done(((bf16[1,128,512]{2,1,0:T(8,128)(2,1)}), bf16[1,1024,512]{2,1,0:T(8,128)(2,1)}) %all-gather.10.cloned.1.call-update) | async-done | bytes 1048592 | tf_op jit(solution)/shard_map/all_gather | solution.py:79
  51.2 27.0 %conditional.2 = (f32[2,256,512]{2,1,0:T(8,128)S(1)}) conditional(s32[]{:T(128)} %convert_element_type.91, () %tuple.25, (f32[2,16,256,512]{3,2,1,0:T(8,128)}, s32[]{:T(128)}, bf16[1024,512]{1,0:T(8,128)(2,1)}, f32[256,128]{1,0:T(8,128)}) %tuple.88), branch_computations={%region_0.1_spmd, %region_1.4_spmd} | conditional | flops 1623326720 | bytes 141476128 | solution.py:101
  51.2 4.4 slice.174
  55.6 1.3 dynamic-slice_bitcast_fusion.1
  57.2 1.6 slice.272
  58.8 3.8 fusion.87
  62.6 3.1 convolution_bitcast_fusion
  65.8 7.3 %reverse_multiply_fusion.1 = (f32[8,127,512]{2,1,0:T(8,128)}, f32[8,127,512]{2,1,0:T(8,128)S(1)}, f32[8,127,512]{2,1,0:T(8,128)}, f32[8,127,512]{2,1,0:T(8,128)}) fusion(f32[8,127,512]{2,1,0:T(8,128)S(1)} %copy-done.12, f32[8,256,512]{2,1,0:T(8,128)S(1)} %convolution_bitcast_fusion, f32[8,127,512]{2,1,0:T(8,128)} %get-tuple-element.115, ...), kind=kLoop, calls=%fused_computation.14 | loop fusion | flops 4161536 | bytes 20807680 | tf_op jit(solution)/shard_map/cond/branch_1_fun/mul | solution.py:48
  73.1 3.8 fusion
  78.2 1.4 fusion.24
  79.6 1.7 fusion.27
  81.5 37.6 %all-gather.12.cloned.1.call-done = bf16[1,1024,512]{1,2,0:T(8,128)(2,1)} async-done(((bf16[1,128,512]{1,2,0:T(8,128)(2,1)}), bf16[1,1024,512]{1,2,0:T(8,128)(2,1)}) %all-gather.12.cloned.1.call-update) | async-done | bytes 1048592 | tf_op jit(solution)/shard_map/all_gather | solution.py:79
  119.2 32.5 %conditional.3 = (f32[2,256,512]{2,1,0:T(8,128)S(1)}) conditional(s32[]{:T(128)} %convert_element_type.91, () %tuple.24, (f32[2,16,256,512]{3,2,1,0:T(8,128)}, s32[]{:T(128)}, bf16[1024,512]{0,1:T(8,128)(2,1)}, f32[256,128]{1,0:T(8,128)}) %tuple.87), branch_computations={%region_4.5_spmd, %region_5.8_spmd} | conditional | flops 1623326720 | bytes 147833088 | solution.py:101
  119.2 1.5 copy.25
  120.7 2.9 convolution_bitcast_fusion.1
  123.6 4.4 slice.190
  128.0 3.1 dynamic-slice_bitcast_fusion.3
  131.4 1.9 copy-done.7
  133.3 1.6 slice.281
  134.9 3.8 fusion.89
  138.7 7.9 %reverse_multiply_fusion.3 = (f32[8,127,512]{2,1,0:T(8,128)}, f32[8,127,512]{2,1,0:T(8,128)S(1)}, f32[8,127,512]{2,1,0:T(8,128)}, f32[8,127,512]{2,1,0:T(8,128)}) fusion(f32[8,127,512]{2,1,0:T(8,128)} %get-tuple-element.130, f32[8,256,512]{2,1,0:T(8,128)S(1)} %convolution_bitcast_fusion.1, f32[8,127,512]{2,1,0:T(8,128)} %get-tuple-element.131, ...), kind=kLoop, calls=%fused_computation.32 | loop fusion | flops 4161536 | bytes 20807680 | tf_op jit(solution)/shard_map/cond/branch_1_fun/mul | solution.py:48
  146.6 3.8 fusion.3
  151.7 1.0 fusion.23
  152.7 1.2 convolution_add_fusion
  153.9 2.1 convolution_convert_fusion
  156.0 1.0 fusion.42
  157.1 8.2 %slice_bitcast_fusion = (f32[8,256,512]{2,1,0:T(8,128)}, f32[8,256,512]{2,1,0:T(8,128)}) fusion(f32[2,8,256,512]{3,2,1,0:T(8,128)} %copy-done.2), kind=kLoop, calls=%fused_computation.50 | loop fusion | bytes 16777216 | tf_op jit(solution)/shard_map/slice | solution.py:107
  165.9 4.5 convolution_bitcast_fusion.3
  170.4 69.5 %reduce-scatter.8.cloned.1.call-done = bf16[16,512]{1,0:T(8,128)(2,1)} async-done(((bf16[512,512]{1,0:T(8,128)(2,1)}), bf16[16,512]{1,0:T(8,128)(2,1)}) %reduce-scatter.8.cloned.1.call-update) | async-done | bytes 16400 | tf_op jit(solution)/shard_map/reduce_scatter | solution.py:162
  239.9 1.5 copy.39
  241.5 39.6 %all-gather.8.cloned.1.call-done = bf16[1024,512]{0,1:T(8,128)(2,1)} async-done(((bf16[128,512]{0,1:T(8,128)(2,1)}), bf16[1024,512]{0,1:T(8,128)(2,1)}) %all-gather.8.cloned.1.call-update) | async-done | bytes 1048592 | tf_op jit(solution)/shard_map/all_gather | solution.py:110
  281.1 1.5 copy.36
  282.6 2.6 convolution_bitcast_fusion.6
  285.8 1.1 multiply_add_fusion.5
  286.9 1.1 copy-done.4
  288.0 1.3 copy-done.6
  289.3 3.8 fusion.17
  293.1 3.7 fusion.9
  296.8 3.8 maximum_reduce_fusion.4
  300.5 1.7 multiply_convert_fusion
  302.6 5.1 %convolution_bitcast_fusion.4 = f32[8,256,512]{2,1,0:T(8,128)} fusion(bf16[8,128,512]{2,1,0:T(8,128)(2,1)S(1)} %bitcast.158, s32[256]{0:T(256)} %copy-done.28, pred[256]{0:T(512)(128)(4,1)} %copy-done.30), kind=kOutput, calls=%fused_computation.68 | convolution fusion | flops 1611104256 | bytes 5244160 | tf_op jit(solution)/shard_map/fb,...bd->...fd/dot_general | solution.py:32
  308.5 0.9 fusion.19
  309.4 10.1 %reduce-scatter.10.cloned.1.call-done = bf16[64,16]{1,0:T(8,128)(2,1)} async-done(((bf16[512,16]{1,0:T(8,128)(2,1)}), bf16[64,16]{1,0:T(8,128)(2,1)}) %reduce-scatter.10.cloned.1.call-update) | async-done | bytes 2064
  319.5 0.8 copy.40
  320.3 1.0 fusion.22
  321.3 38.3 %all-gather.14.cloned.1.call-done = bf16[1,1024,512]{1,2,0:T(8,128)(2,1)} async-done(((bf16[1,128,512]{1,2,0:T(8,128)(2,1)}), bf16[1,1024,512]{1,2,0:T(8,128)(2,1)}) %all-gather.14.cloned.1.call-update) | async-done | bytes 1048592 | tf_op jit(solution)/shard_map/all_gather | solution.py:110
  359.6 1.5 copy.37
  361.1 2.6 convolution_bitcast_fusion.5
  364.4 1.1 multiply_add_fusion.4
  365.5 1.1 copy-done.3
  366.6 1.3 copy-done.5
  367.9 3.1 fusion.16
  370.9 4.4 fusion.8
  375.9 1.0 fusion.21
  379.1 3.0 maximum_reduce_fusion.5
  382.1 1.0 fusion.20
  383.1 0.8 copy.31
  383.8 72.5 %reduce-scatter.6.cloned.1.call-done = bf16[2,128,16]{1,2,0:T(8,128)(2,1)} async-done(((bf16[2,128,512]{1,2,0:T(8,128)(2,1)}), bf16[2,128,16]{1,2,0:T(8,128)(2,1)}) %reduce-scatter.6.cloned.1.call-update) | async-done | bytes 8208 | tf_op jit(solution)/shard_map/reduce_scatter | solution.py:157
  456.3 1.3 convert_multiply_fusion.3
  (104 shorter events, 10.1 us)
Async XLA Ops:
  7.2 2.0 copy-start
  7.2 44.0 %all-gather.10.cloned.1.call-start = ((), (), s32[]{:S(2)}) async-start(), calls=%async_computation.6 | async-start | bytes 1179648 | tf_op jit(solution)/shard_map/all_gather | solution.py:79
  7.9 111.3 %all-gather.12.cloned.1.call-start = ((), (), s32[]{:S(2)}) async-start(), calls=%async_computation.7 | async-start | bytes 1179648 | tf_op jit(solution)/shard_map/all_gather | solution.py:79
  9.0 70.6 %copy-start.21 = (bf16[1,128,512]{1,2,0:T(8,128)(2,1)}, bf16[1,128,512]{1,2,0:T(8,128)(2,1)S(1)}, u32[]{:S(2)}) copy-start(bf16[1,128,512]{1,2,0:T(8,128)(2,1)S(1)} %copy.24) | copy-start | bytes 393220
  9.0 273.6 %copy-start.30 = (pred[256]{0:T(512)(128)(4,1)}, pred[256]{0:T(512)(128)(4,1)S(1)}, u32[]{:S(2)}) copy-start(pred[256]{0:T(512)(128)(4,1)S(1)} %iota_compare_fusion) | copy-start | bytes 772
  9.1 273.5 %copy-start.28 = (s32[256]{0:T(256)}, s32[256]{0:T(256)S(1)}, u32[]{:S(2)}) copy-start(s32[256]{0:T(256)S(1)} %get-tuple-element.103) | copy-start | bytes 3076
  9.1 276.7 %copy-start.32 = (f32[256]{0:T(256)}, f32[256]{0:T(256)S(1)}, u32[]{:S(2)}) copy-start(f32[256]{0:T(256)S(1)} %get-tuple-element.102) | copy-start | bytes 3076
  13.1 8.3 %copy-start.2 = (f32[2,8,256,512]{3,2,1,0:T(8,128)}, f32[2,8,256,512]{3,2,1,0:T(8,128)S(1)}, u32[]{:S(2)}) copy-start(f32[2,8,256,512]{3,2,1,0:T(8,128)S(1)} %convolution_bitcast_fusion.2) | copy-start | bytes 25165828
  58.8 3.8 copy-start.17
  62.6 3.1 copy-start.12
  65.8 7.3 %copy-start.8 = (f32[8,129,512]{2,1,0:T(8,128)S(1)}, f32[8,129,512]{2,1,0:T(8,128)}, u32[]{:S(2)}) copy-start(f32[8,129,512]{2,1,0:T(8,128)} %slice.272) | copy-start | bytes 6340612 | tf_op jit(solution)/shard_map/cond
  73.1 3.8 copy-start.10
  78.2 3.2 copy-start.27
  81.3 158.6 %reduce-scatter.8.cloned.1.call-start = ((), (), s32[]{:S(2)}) async-start(), calls=%async_computation.5 | async-start | bytes 540672 | tf_op jit(solution)/shard_map/reduce_scatter | solution.py:162
  131.1 2.2 copy-start.7
  138.7 7.9 %copy-start.9 = (f32[8,129,512]{2,1,0:T(8,128)S(1)}, f32[8,129,512]{2,1,0:T(8,128)}, u32[]{:S(2)}) copy-start(f32[8,129,512]{2,1,0:T(8,128)} %slice.281) | copy-start | bytes 6340612 | tf_op jit(solution)/shard_map/cond
  146.6 3.8 copy-start.11
  151.7 4.4 copy-start.19
  151.7 4.4 copy-start.26
  153.9 3.3 copy-start.14
  156.0 125.1 %all-gather.8.cloned.1.call-start = ((), (), s32[]{:S(2)}) async-start(), calls=%async_computation.3 | async-start | bytes 1179648 | tf_op jit(solution)/shard_map/all_gather | solution.py:110
  157.1 162.4 %reduce-scatter.10.cloned.1.call-start = ((), (), s32[]{:S(2)}) async-start(), calls=%async_computation.9 | async-start | bytes 147456
  157.1 8.2 %copy-start.13 = (bf16[1,1024,512]{1,2,0:T(8,128)(2,1)S(1)}, bf16[1,1024,512]{1,2,0:T(8,128)(2,1)}, u32[]{:S(2)}) copy-start(bf16[1,1024,512]{1,2,0:T(8,128)(2,1)} %all-gather.12.cloned.1.call-done) | copy-start | bytes 3145732
  241.4 118.1 %all-gather.14.cloned.1.call-start = ((), (), s32[]{:S(2)}) async-start(), calls=%async_computation.8 | async-start | bytes 1179648 | tf_op jit(solution)/shard_map/all_gather | solution.py:110
  285.8 2.2 copy-start.4
  285.8 3.5 copy-start.6
  296.8 3.8 copy-start.22
  296.8 3.8 copy-start.23
  296.8 5.8 %copy-start.16 = (bf16[1,1024,512]{2,1,0:T(8,128)(2,1)S(1)}, bf16[1,1024,512]{2,1,0:T(8,128)(2,1)}, u32[]{:S(2)}) copy-start(bf16[1,1024,512]{2,1,0:T(8,128)(2,1)} %all-gather.10.cloned.1.call-done) | copy-start | bytes 3145732
  302.3 154.0 %reduce-scatter.6.cloned.1.call-start = ((), (), s32[]{:S(2)}) async-start(), calls=%async_computation.4 | async-start | bytes 270336 | tf_op jit(solution)/shard_map/reduce_scatter | solution.py:157
  302.5 5.2 %copy-start.24 = (bf16[1,128,512]{1,2,0:T(8,128)(2,1)S(1)}, bf16[1,128,512]{1,2,0:T(8,128)(2,1)}, u32[]{:S(2)}) copy-start(bf16[1,128,512]{1,2,0:T(8,128)(2,1)} %get-tuple-element.154) | copy-start | bytes 393220
  302.6 6.0 %copy-start.15 = (f32[512,128]{1,0:T(8,128)S(1)}, f32[512,128]{1,0:T(8,128)}, u32[]{:S(2)}) copy-start(f32[512,128]{1,0:T(8,128)} %copy-done.14) | copy-start | bytes 786436
  302.6 6.0 %copy-start.20 = (bf16[512,512]{1,0:T(8,128)(2,1)S(1)}, bf16[512,512]{1,0:T(8,128)(2,1)}, u32[]{:S(2)}) copy-start(bf16[512,512]{1,0:T(8,128)(2,1)} %param.14) | copy-start | bytes 1572868
  302.6 17.7 %copy-start.18 = (f32[256,512]{1,0:T(8,128)S(1)}, f32[256,512]{1,0:T(8,128)}, u32[]{:S(2)}) copy-start(f32[256,512]{1,0:T(8,128)} %get-tuple-element.161) | copy-start | bytes 1572868
  307.7 53.3 %copy-start.29 = (s32[256]{0:T(256)S(1)}, s32[256]{0:T(256)}, u32[]{:S(2)}) copy-start(s32[256]{0:T(256)} %copy-done.28) | copy-start | bytes 3076
  307.7 53.3 %copy-start.31 = (pred[256]{0:T(512)(128)(4,1)S(1)}, pred[256]{0:T(512)(128)(4,1)}, u32[]{:S(2)}) copy-start(pred[256]{0:T(512)(128)(4,1)} %copy-done.30) | copy-start | bytes 772
  363.7 0.7 copy-start.33
  364.4 2.2 copy-start.3
  364.4 3.5 copy-start.5
  375.3 3.0 copy-start.25
  379.1 78.6 %copy-start.1 = (bf16[2,1024,512]{2,1,0:T(8,128)(2,1)S(1)}, bf16[2,1024,512]{2,1,0:T(8,128)(2,1)}, u32[]{:S(2)}) copy-start(bf16[2,1024,512]{2,1,0:T(8,128)(2,1)} %param.13) | copy-start | bytes 6291460
Sparse Core Ops, SparseCore 0:
  9.8 41.3 all-gather.9
  81.5 37.6 all-gather.11
  156.1 83.7 reduce-scatter.7
  242.1 38.9 all-gather.7
  283.4 36.0 reduce-scatter.9
  321.6 37.8 all-gather.13
  377.8 78.4 reduce-scatter.5
where the time goes:
time: 469 us; the launch traced here: 465 us
  waiting for transfers between devices  296 us (63%)
  local copies, waits for them, and re-layouts  59.8 us (13%)
  other arithmetic  54.6 us (12%)
  matrix products  39 us (8%)
  between operations  14.8 us (3%)
    all_gather x2, waiting for transfers between devices, anti_owner(): lax.all_gather(grad_rows, 'ctx', axis=0, tiled=True)  77.9 us
    reduce_scatter x1, waiting for transfers between devices, on_device(): lax.psum_scatter(own_lags.astype(jnp.bfloat16), 'dp', scatter_dimension=2...  72.5 us
    reduce_scatter x1, waiting for transfers between devices, on_device(): lax.psum_scatter(lax.dot_general(gated, cotangent, (((0,), (0,)), ((), ()...  69.5 us
    all_gather x2, waiting for transfers between devices, causal(): piece = lax.all_gather(source, 'ctx', axis=0, tiled=True)  65.1 us
    dot_general x7, matrix products, to_spectra(): jnp.einsum('fb,...bd->...fd', table, blocks.astype(jnp.float32), precisio...  25 us
    mul x4, other arithmetic, spectral_product(): cross = left_imag * right_imag  22 us
    sub x4, other arithmetic, spectral_product(): left_real * right_real - jnp.concatenate([border, cross, border], axis=-2)  15.5 us
    unnamed x61, local copies, waits for them, and re-layouts  10.9 us
  transfers between devices with their start and end apart: 7, of which 7 were waited for; matrix products, arithmetic and copies ran while one was open for 14% of the time, Pallas kernels for 0%

commit v1 on v0

--- a/solution.py
+++ b/solution.py
@@ -76,7 +76,9 @@
 
     def causal(source, padded_filter):
         initial = jnp.zeros((own_blocks + 1, 2 * block, width), jnp.float32)
-        piece = lax.all_gather(source, "ctx", axis=0, tiled=True)
+        piece = jnp.concatenate(
+            lax.all_to_all(jnp.stack([source] * lax.axis_size("ctx")), "ctx", 0, 0), axis=0
+        )
         start = jnp.int32(0)
 
         def work(total):

time: 469 us -> 430 us (0.917)
  waiting for transfers between devices: 296 us -> 231 us
  starting transfers between devices: 0.5 us -> 12.7 us
  local copies, waits for them, and re-layouts: 59.8 us -> 70.8 us
    all_gather x2, waiting for transfers between devices: 65.1 us -> 0.02 us  [anti_owner(): lax.all_gather(source, 'ctx', axis=0, tiled=True)]
    all_to_all x0 -> x2, waiting for transfers between devices: none -> 44.8 us  [causal(): lax.all_to_all(jnp.stack([source] * lax.axis_size('ctx')), 'ctx', 0, 0)]
    all_gather x2, waiting for transfers between devices: 77.9 us -> 38.3 us  [anti_owner(): lax.all_gather(grad_rows, 'ctx', axis=0, tiled=True)]
    all_to_all x0 -> x2, starting transfers between devices: none -> 12 us  [causal(): lax.all_to_all(jnp.stack([source] * lax.axis_size('ctx')), 'ctx', 0, 0)]
    slice x2, local copies, waits for them, and re-layouts: 7.57 us -> 12.7 us  [spectral_product(): left_imag = left[..., block + 1:, :]]
    unnamed x61 -> x43, local copies, waits for them, and re-layouts: 10.9 us -> 9.86 us
  transfers between devices with their start and end apart: 7 -> 9, of which waited for: 7 -> 6; matrix products, arithmetic and copies ran while one was open for 14% -> 24% of each run, Pallas kernels for 0% -> 0%
where the time goes in v1:
time: 430 us; the launch traced here: 425 us
  waiting for transfers between devices  231 us (54%)
  local copies, waits for them, and re-layouts  70.8 us (16%)
  other arithmetic  55.2 us (13%)
  matrix products  39.1 us (9%)
  between operations  15.9 us (4%)
  starting transfers between devices  12.7 us (3%)
    reduce_scatter x1, waiting for transfers between devices, on_device(): lax.psum_scatter(own_lags.astype(jnp.bfloat16), 'dp', scatter_dimension=2...  72.5 us
    reduce_scatter x1, waiting for transfers between devices, on_device(): lax.psum_scatter(lax.dot_general(gated, cotangent, (((0,), (0,)), ((), ()...  65 us
    all_to_all x2, waiting for transfers between devices, causal(): lax.all_to_all(jnp.stack([source] * lax.axis_size('ctx')), 'ctx', 0, 0)  44.8 us
    all_gather x2, waiting for transfers between devices, anti_owner(): lax.all_gather(grad_rows, 'ctx', axis=0, tiled=True)  38.3 us
    dot_general x7, matrix products, to_spectra(): jnp.einsum('fb,...bd->...fd', table, blocks.astype(jnp.float32), precisio...  25.4 us
    mul x4, other arithmetic, spectral_product(): cross = left_imag * right_imag  22 us
    sub x4, other arithmetic, spectral_product(): left_real * right_real - jnp.concatenate([border, cross, border], axis=-2)  13.7 us
    slice x2, local copies, waits for them, and re-layouts, spectral_product(): left_imag = left[..., block + 1:, :]  12.7 us
  transfers between devices with their start and end apart: 9, of which 6 were waited for; matrix products, arithmetic and copies ran while one was open for 24% of the time, Pallas kernels for 0%

profile of v1, /device:TPU:2, one launch (start us, length us, event | category | flops | bytes accessed | tf_op | source)
XLA Modules:
  0.0 424.8 jit_solution(5188274380071441472)
XLA Ops:
  8.0 2.2 stack.34
  10.2 8.5 %all-to-all-start = ((bf16[8,128,512]{2,1,0:T(8,128)(2,1)}), bf16[8,128,512]{2,1,0:T(8,128)(2,1)S(1)}, u32[]{:S(2)}, u32[]{:S(2)}) async-start(bf16[8,128,512]{2,1,0:T(8,128)(2,1)} %stack.34), calls=%async_computation | async-start | bytes 2097152 | tf_op jit(solution)/shard_map/all_to_all | solution.py:80
  18.9 3.9 convolution_bitcast_fusion.2
  22.9 8.0 %concatenate.92 = f32[2,16,256,512]{3,2,1,0:T(8,128)} pad(f32[2,8,256,512]{3,2,1,0:T(8,128)S(1)} %convolution_bitcast_fusion.2, f32[]{:T(128)} %constant.162.clone.1), padding=0_0x8_0x0_0x0_0 | pad | bytes 25165828 | tf_op jit(solution)/shard_map/concatenate | solution.py:71
  31.2 1.3 cosine_select_fusion
  32.4 1.1 select_multiply_fusion
  33.5 13.9 %all-to-all-done = bf16[8,128,512]{2,1,0:T(8,128)(2,1)S(1)} async-done(((bf16[8,128,512]{2,1,0:T(8,128)(2,1)}), bf16[8,128,512]{2,1,0:T(8,128)(2,1)S(1)}, u32[]{:S(2)}, u32[]{:S(2)}) %all-to-all-start) | async-done | bytes 1048608 | tf_op jit(solution)/shard_map/all_to_all | solution.py:80
  47.4 34.2 %conditional.2 = (f32[2,256,512]{2,1,0:T(8,128)S(1)}) conditional(s32[]{:T(128)} %convert_element_type.91, () %tuple.25, (f32[2,16,256,512]{3,2,1,0:T(8,128)}, s32[]{:T(128)}, bf16[8,128,512]{2,1,0:T(8,128)(2,1)S(1)}, f32[256,128]{1,0:T(8,128)}) %tuple.26), branch_computations={%region_0.1_spmd, %region_1.4_spmd} | conditional | flops 1623326720 | bytes 128827608 | solution.py:103
  47.4 4.4 %slice.174 = f32[1,16,256,512]{3,2,1,0:T(8,128)S(1)} slice(f32[2,16,256,512]{3,2,1,0:T(8,128)} %get-tuple-element.61), slice={[0:1], [0:16], [0:256], [0:512]} | slice | bytes 16777216 | tf_op jit(solution)/shard_map/slice | solution.py:142
  51.8 3.0 dynamic-slice_bitcast_fusion.1
  54.9 6.3 %fusion.87 = (f32[8,127,512]{2,1,0:T(8,128)}, f32[8,127,512]{2,1,0:T(8,128)}, f32[8,127,512]{2,1,0:T(8,128)}, f32[8,127,512]{2,1,0:T(8,128)}) fusion(f32[8,256,512]{2,1,0:T(8,128)} %get-tuple-element.96, f32[8,256,512]{2,1,0:T(8,128)S(1)} %get-tuple-element.97), kind=kLoop, calls=%fused_computation.191 | loop fusion | bytes 16646144 | tf_op jit(solution)/shard_map/cond/branch_1_fun/slice | solution.py:43
  61.2 3.0 convolution_bitcast_fusion
  64.2 7.5 %reverse_multiply_fusion.1 = (f32[8,127,512]{2,1,0:T(8,128)}, f32[8,127,512]{2,1,0:T(8,128)S(1)}, f32[8,127,512]{2,1,0:T(8,128)S(1)}, f32[8,127,512]{2,1,0:T(8,128)}) fusion(f32[8,127,512]{2,1,0:T(8,128)} %get-tuple-element.106, f32[8,256,512]{2,1,0:T(8,128)S(1)} %convolution_bitcast_fusion, f32[8,127,512]{2,1,0:T(8,128)} %get-tuple-element.107, ...), kind=kLoop, calls=%fused_computation.14 | loop fusion | flops 4161536 | bytes 20807680 | tf_op jit(solution)/shard_map/cond/branch_1_fun/mul | solution.py:48
  71.7 1.8 slice.266
  73.9 1.3 copy-done.7
  75.8 2.8 fusion
  79.3 2.2 maximum_reduce_fusion.1
  81.6 1.4 fusion.24
  83.0 1.7 fusion.27
  84.8 1.1 stack.36
  85.9 3.6 all-to-all-start.1
  90.4 30.9 %all-to-all-done.1 = bf16[8,128,512]{2,1,0:T(8,128)(2,1)S(1)} async-done(((bf16[8,128,512]{2,1,0:T(8,128)(2,1)}), bf16[8,128,512]{2,1,0:T(8,128)(2,1)S(1)}, u32[]{:S(2)}, u32[]{:S(2)}) %all-to-all-start.1) | async-done | bytes 1048608 | tf_op jit(solution)/shard_map/all_to_all | solution.py:80
  121.4 34.3 %conditional.3 = (f32[2,256,512]{2,1,0:T(8,128)S(1)}) conditional(s32[]{:T(128)} %convert_element_type.91, () %tuple.24, (f32[2,16,256,512]{3,2,1,0:T(8,128)}, s32[]{:T(128)}, bf16[8,128,512]{2,1,0:T(8,128)(2,1)S(1)}, f32[256,128]{1,0:T(8,128)}) %tuple.27), branch_computations={%region_4.5_spmd, %region_5.8_spmd} | conditional | flops 1623326720 | bytes 128827608 | solution.py:103
  121.4 4.4 %slice.190 = f32[1,16,256,512]{3,2,1,0:T(8,128)S(1)} slice(f32[2,16,256,512]{3,2,1,0:T(8,128)} %get-tuple-element.72), slice={[1:2], [0:16], [0:256], [0:512]} | slice | bytes 16777216 | tf_op jit(solution)/shard_map/slice | solution.py:144
  125.8 3.0 dynamic-slice_bitcast_fusion.3
  128.9 6.4 %fusion.89 = (f32[8,127,512]{2,1,0:T(8,128)}, f32[8,127,512]{2,1,0:T(8,128)}, f32[8,127,512]{2,1,0:T(8,128)}, f32[8,127,512]{2,1,0:T(8,128)}) fusion(f32[8,256,512]{2,1,0:T(8,128)} %get-tuple-element.112, f32[8,256,512]{2,1,0:T(8,128)S(1)} %get-tuple-element.113), kind=kLoop, calls=%fused_computation.193 | loop fusion | bytes 16646144 | tf_op jit(solution)/shard_map/cond/branch_1_fun/slice | solution.py:43
  135.3 3.0 convolution_bitcast_fusion.1
  138.2 7.5 %reverse_multiply_fusion.3 = (f32[8,127,512]{2,1,0:T(8,128)}, f32[8,127,512]{2,1,0:T(8,128)S(1)}, f32[8,127,512]{2,1,0:T(8,128)S(1)}, f32[8,127,512]{2,1,0:T(8,128)}) fusion(f32[8,127,512]{2,1,0:T(8,128)} %get-tuple-element.122, f32[8,256,512]{2,1,0:T(8,128)S(1)} %convolution_bitcast_fusion.1, f32[8,127,512]{2,1,0:T(8,128)} %get-tuple-element.123, ...), kind=kLoop, calls=%fused_computation.32 | loop fusion | flops 4161536 | bytes 20807680 | tf_op jit(solution)/shard_map/cond/branch_1_fun/mul | solution.py:48
  145.8 1.8 slice.275
  148.0 1.3 copy-done.9
  149.9 2.8 fusion.3
  153.3 2.2 maximum_reduce_fusion.3
  156.7 1.0 convolution_add_fusion
  157.7 2.1 convolution_convert_fusion
  161.8 8.2 %slice_bitcast_fusion = (f32[8,256,512]{2,1,0:T(8,128)}, f32[8,256,512]{2,1,0:T(8,128)}) fusion(f32[2,8,256,512]{3,2,1,0:T(8,128)} %copy-done.2), kind=kLoop, calls=%fused_computation.50 | loop fusion | bytes 16777216 | tf_op jit(solution)/shard_map/slice | solution.py:109
  170.0 1.5 copy.38
  171.5 4.5 %convolution_bitcast_fusion.3 = f32[8,256,512]{2,1,0:T(8,128)} fusion(bf16[8,128,512]{2,1,0:T(8,128)(2,1)S(1)} %bitcast.151, s32[256]{0:T(256)S(1)} %get-tuple-element.95, pred[256]{0:T(512)(128)(4,1)S(1)} %iota_compare_fusion), kind=kOutput, calls=%fused_computation.67 | convolution fusion | flops 1611104256 | bytes 5244160 | tf_op jit(solution)/shard_map/fb,...bd->...fd/dot_general | solution.py:32
  176.0 65.0 %reduce-scatter.8.cloned.1.call-done = bf16[16,512]{1,0:T(8,128)(2,1)} async-done(((bf16[512,512]{1,0:T(8,128)(2,1)}), bf16[16,512]{1,0:T(8,128)(2,1)}) %reduce-scatter.8.cloned.1.call-update) | async-done | bytes 16400 | tf_op jit(solution)/shard_map/reduce_scatter | solution.py:164
  241.1 1.5 copy.39
  242.6 1.5 copy.36
  244.2 2.6 convolution_bitcast_fusion.6
  247.4 1.1 multiply_add_fusion.5
  248.5 1.1 copy-done.4
  249.5 1.3 copy-done.6
  250.8 3.8 fusion.17
  254.6 3.6 fusion.9
  258.3 2.9 maximum_reduce_fusion.4
  261.2 1.7 multiply_convert_fusion
  263.2 5.7 %convolution_bitcast_fusion.4 = f32[8,256,512]{2,1,0:T(8,128)} fusion(bf16[8,128,512]{2,1,0:T(8,128)(2,1)} %bitcast.156, s32[256]{0:T(256)S(1)} %get-tuple-element.95, pred[256]{0:T(512)(128)(4,1)S(1)} %iota_compare_fusion), kind=kOutput, calls=%fused_computation.68 | convolution fusion | flops 1611104256 | bytes 5244160 | tf_op jit(solution)/shard_map/fb,...bd->...fd/dot_general | solution.py:32
  270.6 8.9 %reduce-scatter.10.cloned.1.call-done = bf16[64,16]{1,0:T(8,128)(2,1)} async-done(((bf16[512,16]{1,0:T(8,128)(2,1)}), bf16[64,16]{1,0:T(8,128)(2,1)}) %reduce-scatter.10.cloned.1.call-update) | async-done | bytes 2064
  280.3 1.0 fusion.22
  281.3 38.3 %all-gather.10.cloned.1.call-done = bf16[1,1024,512]{1,2,0:T(8,128)(2,1)} async-done(((bf16[1,128,512]{1,2,0:T(8,128)(2,1)}), bf16[1,1024,512]{1,2,0:T(8,128)(2,1)}) %all-gather.10.cloned.1.call-update) | async-done | bytes 1048592 | tf_op jit(solution)/shard_map/all_gather | solution.py:112
  319.6 1.5 copy.37
  321.1 2.6 convolution_bitcast_fusion.5
  324.3 1.1 multiply_add_fusion.4
  325.4 1.1 copy-done.3
  326.5 1.3 copy-done.5
  327.7 3.1 fusion.16
  330.8 4.4 %fusion.8 = (f32[8,129,512]{2,1,0:T(8,128)S(1)}, f32[8,129,512]{2,1,0:T(8,128)}) fusion(f32[8,1,512]{2,1,0:T(1,128)S(1)} %broadcast.149, f32[8,256,512]{2,1,0:T(8,128)S(1)} %copy-done.3, f32[8,127,512]{2,1,0:T(8,128)S(1)} %get-tuple-element.128, s32[]{:T(128)S(6)} %select_n.74, f32[8,256,512]{2,1,0:T(8,128)S(1)} %multiply_add_fusion.4, ...), kind=kLoop, calls=%fused_computation.61 | loop fusion | flops 4227072 | bytes 16826372 | tf_op jit(solution)/shard_map/while/body/eval_jaxpr/sub | solution.py:50
  335.8 1.0 fusion.21
  338.9 3.0 maximum_reduce_fusion.5
  342.0 1.0 fusion.20
  343.7 72.5 %reduce-scatter.6.cloned.1.call-done = bf16[2,128,16]{1,2,0:T(8,128)(2,1)} async-done(((bf16[2,128,512]{1,2,0:T(8,128)(2,1)}), bf16[2,128,16]{1,2,0:T(8,128)(2,1)}) %reduce-scatter.6.cloned.1.call-update) | async-done | bytes 8208 | tf_op jit(solution)/shard_map/reduce_scatter | solution.py:159
  416.2 1.3 convert_multiply_fusion.3
  (86 shorter events, 15.1 us)
Async XLA Ops:
  8.0 10.9 %copy-start = (bf16[2,1024,512]{2,1,0:T(8,128)(2,1)S(1)}, bf16[2,1024,512]{2,1,0:T(8,128)(2,1)}, u32[]{:S(2)}) copy-start(bf16[2,1024,512]{2,1,0:T(8,128)(2,1)} %param.13) | copy-start | bytes 6291460
  8.0 10.7 %copy-start.20 = (bf16[1,128,512]{2,1,0:T(8,128)(2,1)S(1)}, bf16[1,128,512]{2,1,0:T(8,128)(2,1)}, u32[]{:S(2)}) copy-start(bf16[1,128,512]{2,1,0:T(8,128)(2,1)} %param.11) | copy-start | bytes 393220
  10.2 37.2 %all-to-all-start = ((bf16[8,128,512]{2,1,0:T(8,128)(2,1)}), bf16[8,128,512]{2,1,0:T(8,128)(2,1)S(1)}, u32[]{:S(2)}, u32[]{:S(2)}) async-start(bf16[8,128,512]{2,1,0:T(8,128)(2,1)} %stack.34), calls=%async_computation | async-start | bytes 2097152 | tf_op jit(solution)/shard_map/all_to_all | solution.py:80
  18.8 64.2 %copy-start.15 = (bf16[1,128,512]{1,2,0:T(8,128)(2,1)}, bf16[1,128,512]{1,2,0:T(8,128)(2,1)S(1)}, u32[]{:S(2)}) copy-start(bf16[1,128,512]{1,2,0:T(8,128)(2,1)S(1)} %copy.24) | copy-start | bytes 393220
  22.9 8.3 %copy-start.2 = (f32[2,8,256,512]{3,2,1,0:T(8,128)}, f32[2,8,256,512]{3,2,1,0:T(8,128)S(1)}, u32[]{:S(2)}) copy-start(f32[2,8,256,512]{3,2,1,0:T(8,128)S(1)} %convolution_bitcast_fusion.2) | copy-start | bytes 25165828
  73.6 1.6 copy-start.7
  73.6 2.2 copy-start.8
  83.0 7.3 %copy-start.21 = (bf16[1,128,512]{2,1,0:T(8,128)(2,1)S(1)}, bf16[1,128,512]{2,1,0:T(8,128)(2,1)}, u32[]{:S(2)}) copy-start(bf16[1,128,512]{2,1,0:T(8,128)(2,1)} %param.12) | copy-start | bytes 393220
  84.7 4.8 %copy-start.17 = (bf16[1,128,512]{1,2,0:T(8,128)(2,1)}, bf16[1,128,512]{1,2,0:T(8,128)(2,1)S(1)}, u32[]{:S(2)}) copy-start(bf16[1,128,512]{1,2,0:T(8,128)(2,1)S(1)} %get-tuple-element.150) | copy-start | bytes 393220
  85.9 35.4 %all-to-all-start.1 = ((bf16[8,128,512]{2,1,0:T(8,128)(2,1)}), bf16[8,128,512]{2,1,0:T(8,128)(2,1)S(1)}, u32[]{:S(2)}, u32[]{:S(2)}) async-start(bf16[8,128,512]{2,1,0:T(8,128)(2,1)} %stack.36), calls=%async_computation.1 | async-start | bytes 2097152 | tf_op jit(solution)/shard_map/all_to_all | solution.py:80
  89.5 80.5 %all-gather.14.cloned.1.call-start = ((), (), s32[]{:S(2)}) async-start(), calls=%async_computation.10 | async-start | bytes 1179648 | tf_op jit(solution)/shard_map/all_gather | solution.py:111
  90.2 150.8 %reduce-scatter.8.cloned.1.call-start = ((), (), s32[]{:S(2)}) async-start(), calls=%async_computation.7 | async-start | bytes 540672 | tf_op jit(solution)/shard_map/reduce_scatter | solution.py:164
  147.7 1.6 copy-start.9
  147.7 2.2 copy-start.10
  155.7 4.4 %copy-start.13 = (bf16[512,512]{1,0:T(8,128)(2,1)S(1)}, bf16[512,512]{1,0:T(8,128)(2,1)}, u32[]{:S(2)}) copy-start(bf16[512,512]{1,0:T(8,128)(2,1)} %param.14) | copy-start | bytes 1572868
  155.7 4.4 %copy-start.19 = (bf16[1,128,512]{2,1,0:T(8,128)(2,1)S(1)}, bf16[1,128,512]{2,1,0:T(8,128)(2,1)}, u32[]{:S(2)}) copy-start(bf16[1,128,512]{2,1,0:T(8,128)(2,1)} %param.15) | copy-start | bytes 393220
  157.7 12.3 %copy-start.11 = (f32[512,128]{1,0:T(8,128)}, f32[512,128]{1,0:T(8,128)S(1)}, u32[]{:S(2)}) copy-start(f32[512,128]{1,0:T(8,128)S(1)} %convolution_add_fusion) | copy-start | bytes 786436
  159.8 82.8 %all-gather.8.cloned.1.call-start = ((), (), s32[]{:S(2)}) async-start(), calls=%async_computation.5 | async-start | bytes 1179648 | tf_op jit(solution)/shard_map/all_gather | solution.py:112
  161.0 102.2 %all-gather.12.cloned.1.call-start = ((), (), s32[]{:S(2)}) async-start(), calls=%async_computation.9 | async-start | bytes 1179648 | tf_op jit(solution)/shard_map/all_gather | solution.py:111
  161.8 117.7 %reduce-scatter.10.cloned.1.call-start = ((), (), s32[]{:S(2)}) async-start(), calls=%async_computation.11 | async-start | bytes 147456
  242.6 77.0 %all-gather.10.cloned.1.call-start = ((), (), s32[]{:S(2)}) async-start(), calls=%async_computation.8 | async-start | bytes 1179648 | tf_op jit(solution)/shard_map/all_gather | solution.py:112
  247.4 2.2 copy-start.4
  247.4 3.5 copy-start.6
  258.3 2.9 copy-start.16
  258.3 2.9 copy-start.18
  262.9 153.3 %reduce-scatter.6.cloned.1.call-start = ((), (), s32[]{:S(2)}) async-start(), calls=%async_computation.6 | async-start | bytes 270336 | tf_op jit(solution)/shard_map/reduce_scatter | solution.py:159
  263.2 6.4 %copy-start.12 = (f32[512,128]{1,0:T(8,128)S(1)}, f32[512,128]{1,0:T(8,128)}, u32[]{:S(2)}) copy-start(f32[512,128]{1,0:T(8,128)} %copy-done.11) | copy-start | bytes 786436
  263.2 6.4 %copy-start.14 = (bf16[512,512]{1,0:T(8,128)(2,1)S(1)}, bf16[512,512]{1,0:T(8,128)(2,1)}, u32[]{:S(2)}) copy-start(bf16[512,512]{1,0:T(8,128)(2,1)} %param.14) | copy-start | bytes 1572868
  324.3 2.2 copy-start.3
  324.3 3.5 copy-start.5
  338.9 78.6 %copy-start.1 = (bf16[2,1024,512]{2,1,0:T(8,128)(2,1)S(1)}, bf16[2,1024,512]{2,1,0:T(8,128)(2,1)}, u32[]{:S(2)}) copy-start(bf16[2,1024,512]{2,1,0:T(8,128)(2,1)} %param.13) | copy-start | bytes 6291460
Sparse Core Ops, SparseCore 0:
  92.6 46.3 all-gather.13
  162.9 35.6 all-gather.7
  200.4 37.3 all-gather.11
  242.7 36.7 reduce-scatter.9
  281.6 37.9 all-gather.9
Sparse Core Ops, SparseCore 1:
  159.9 81.1 reduce-scatter.7
  337.6 78.5 reduce-scatter.5
